TPU v7x, 512 devices: a whole 4x8x8 slice. The times are simulated.
512 devices in a mesh: mesh: 64 (over x, y, z_lo), state: 8 (over z_hi, core).
Axes of the slice: x: 4, y: 8, z: 8 (z_hi: 4, z_lo: 2; z = z_hi * 2 + z_lo), core: 2. Of those that a mesh axis runs over, the one named last changes fastest.
Arguments:
- subspace: float32 [2048, 16384], P('state', 'mesh'), may hold values from -6 to 6
- ritz: float32 [1024, 2048], P('state'), may hold values from -0.125 to 0.125
- element_ham: float32 [1024, 125, 125], P('mesh'), may hold values from -0.6 to 0.6
- connect: int32 [1024, 125], P('mesh'), may hold values from 0 to 383, as said below
- send_rows: int32 [64, 4, 32], P('mesh'), may hold values from 0 to 255, as said below
Outputs:
- filtered: float32 [1024, 16384], P('state', 'mesh')
Inputs may be any that keep to these rules, and one draw needn't show every extreme that they name: send_rows[p][k] lists nodes of partition p, local numbering, that neighbour k of p uses; only a leading part of each list, of 32 entries or fewer, is used, and some partition uses a whole list. `connect`: entries below 256 are the partition's own nodes; an entry 256 + k * 32 + j is entry j of the list that neighbour k keeps for this partition.
All inputs are finite; a program needn't handle non-finite values.
Results may differ from a plain program's by a relative error of at most 0.0001.
Values sent between devices are 32-bit elements; how exact they have to be, the bound alone decides.
A program may use at most 64 MiB of HBM per device.

v0:
```python
import jax
import jax.numpy as jnp
from jax import lax
from jax.sharding import PartitionSpec as P


def per_device(subspace, ritz, element_ham, connect, send_rows):
    block_rows = ritz.shape[0]
    node_count = subspace.shape[1]
    partitions = lax.axis_size("mesh")
    slot_count = send_rows.shape[1]
    halo_width = send_rows.shape[2]
    across = partitions // 2
    offsets = (1, -1, across, -across)
    start_block = jnp.dot(
        ritz,
        lax.all_gather(subspace, "state", axis=0, tiled=True),
        precision=lax.Precision.HIGHEST,
        preferred_element_type=jnp.float32,
    )
    own_index = lax.axis_index("mesh")
    neighbour_ids = (own_index + jnp.array(offsets, jnp.int32) + partitions) % partitions
    selector = (neighbour_ids[:, None] == jnp.arange(partitions, dtype=jnp.int32)[None, :]).astype(
        jnp.float32
    )
    slot_ids = jnp.arange(4, dtype=jnp.int32)
    parity_ids = jnp.arange(2, dtype=jnp.int32)
    send_parity = ((slot_ids % 2)[:, None] == parity_ids[None, :]).astype(jnp.float32)
    take_parity = (((slot_ids ^ 1) % 2)[:, None] == parity_ids[None, :]).astype(jnp.float32)
    send_route = selector[:, :, None] * send_parity[:, None, :]
    take_route = selector[:, :, None] * take_parity[:, None, :]
    list_rows = send_rows[0].reshape(-1)

    def fetch_ghosts(packed):
        outgoing = jnp.einsum("kpr,ckj->pcrj", send_route, packed, precision=lax.Precision.HIGHEST)
        incoming = lax.all_to_all(
            outgoing.reshape(partitions, block_rows * 2 * halo_width),
            "mesh",
            split_axis=0,
            concat_axis=0,
            tiled=True,
        )
        return jnp.einsum(
            "kpr,pcrj->ckj",
            take_route,
            incoming.reshape(partitions, block_rows, 2, halo_width),
            precision=lax.Precision.HIGHEST,
        )

    def return_sums(returned_part):
        going_back = jnp.einsum(
            "kpr,ckj->pcrj", send_route, returned_part, precision=lax.Precision.HIGHEST
        )
        arrived = lax.all_to_all(
            going_back.reshape(partitions, block_rows * 2 * halo_width),
            "mesh",
            split_axis=0,
            concat_axis=0,
            tiled=True,
        )
        return jnp.einsum(
            "kpr,pcrj->ckj",
            take_route,
            arrived.reshape(partitions, block_rows, 2, halo_width),
            precision=lax.Precision.HIGHEST,
        )

    def apply_ham(values_in):
        packed = values_in[:, list_rows].reshape(block_rows, slot_count, halo_width)
        ghosts = fetch_ghosts(packed)
        extended = jnp.concatenate(
            [values_in, ghosts.reshape(block_rows, slot_count * halo_width)], 1
        )
        element_values = extended[:, connect]
        products = jnp.einsum(
            "eab,ceb->cea", element_ham, element_values, precision=lax.Precision.HIGHEST
        )
        summed = jnp.zeros(extended.shape, jnp.float32).at[:, connect].add(products)
        returned_part = summed[:, node_count:].reshape(block_rows, slot_count, halo_width)
        owner_terms = return_sums(returned_part)
        return (
            summed[:, :node_count]
            .at[:, list_rows]
            .add(owner_terms.reshape(block_rows, slot_count * halo_width))
        )

    half = 1.5
    centre = 2.5
    sigma_one = half / (-1.0 - centre)
    sigma_two = 1.0 / (2.0 / sigma_one - sigma_one)
    first = sigma_one / half * (apply_ham(start_block) - centre * start_block)
    second = 2.0 * sigma_two / half * (apply_ham(first) - centre * first)
    return second - sigma_one * sigma_two * start_block


def solution(mesh):
    in_specs = (
        P("state", "mesh"),
        P("state", None),
        P("mesh", None, None),
        P("mesh", None),
        P("mesh", None, None),
    )
    out_specs = P("state", "mesh")
    return jax.shard_map(
        per_device, mesh=mesh, in_specs=in_specs, out_specs=out_specs, check_vma=False
    )
```

profile of v0, /device:TPU:1, one launch (start us, length us, event | category | flops | bytes accessed | tf_op | source)
XLA Modules:
  0.0 442.9 jit_solution(11730781760586133528)
XLA Ops:
  6.5 0.7 all-gather.2.cloned.1.call-update
  7.3 0.8 reshape_squeeze.3
  8.0 0.7 and_select_fusion.2
  8.8 46.6 %all-gather.2.cloned.1.call-done = f32[2048,256]{1,0:T(8,128)} async-done(((f32[256,256]{1,0:T(8,128)}), f32[2048,256]{1,0:T(8,128)}) %all-gather.2.cloned.1.call-update) | async-done | bytes 2097168 | tf_op jit(solution)/shard_map/all_gather | solution.py:17
  55.4 2.7 fusion.69
  58.2 0.7 gather_fusion
  58.9 1.9 convolution_bitcast_fusion.3
  60.8 4.5 %copy.51 = f32[64,128,2,32]{0,3,2,1:T(8,128)} copy(f32[64,128,2,32]{1,0,2,3:T(8,128)S(1)} %convolution_bitcast_fusion.3) | data formatting | bytes 4194304 | tf_op jit(solution)/shard_map/kpr,ckj->pcrj/transpose | solution.py:35
  65.3 6.8 %copy.52 = f32[64,1,8192]{2,1,0:T(1,128)} copy(f32[64,1,8192]{0,2,1:T(8,128)} %bitcast.92) | data formatting | bytes 4194304 | tf_op jit(solution)/shard_map/all_to_all | solution.py:36
  72.0 10.0 %all-to-all-start = ((f32[64,1,8192]{2,1,0:T(1,128)}), f32[64,1,8192]{2,1,0:T(1,128)S(1)}, u32[]{:S(2)}, u32[]{:S(2)}) async-start(f32[64,1,8192]{2,1,0:T(1,128)} %copy.52), calls=%async_computation | async-start | bytes 4194304 | tf_op jit(solution)/shard_map/all_to_all | solution.py:36
  82.2 49.4 %all-to-all-done = f32[64,1,8192]{2,1,0:T(1,128)S(1)} async-done(((f32[64,1,8192]{2,1,0:T(1,128)}), f32[64,1,8192]{2,1,0:T(1,128)S(1)}, u32[]{:S(2)}, u32[]{:S(2)}) %all-to-all-start) | async-done | bytes 2097184 | tf_op jit(solution)/shard_map/all_to_all | solution.py:36
  131.6 4.5 %copy.53 = f32[64,1,8192]{0,2,1:T(8,128)} copy(f32[64,1,8192]{2,1,0:T(1,128)S(1)} %all-to-all-done) | data formatting | bytes 4194304 | tf_op jit(solution)/shard_map/all_to_all | solution.py:36
  136.0 8.1 %fusion.8 = f32[128,4,32]{0,1,2:T(4,128)S(1)} fusion(f32[64,128,2,32]{0,3,2,1:T(8,128)} %bitcast.97, f32[4,2]{0,1:T(2,128)S(1)} %compare_convert_fusion, f32[4,64]{1,0:T(4,128)S(1)} %fusion.65), kind=kOutput, calls=%fused_computation.22 | convolution fusion | flops 25166336 | bytes 2163744 | tf_op jit(solution)/shard_map/kpr,pcrj->ckj/dot_general | solution.py:43
  144.2 0.1 copy.56
  144.3 0.1 copy.57
  144.5 5.6 %gather_fusion.1 = f32[2000,128]{1,0:T(8,128)S(1)} fusion(f32[128,384]{0,1:T(8,128)S(1)} %copy.57, s32[2048]{0:T(1024)S(1)} %pad_clamp_fusion), kind=kCustom, calls=%fused_computation.1 | custom fusion | bytes 2056000 | tf_op jit(solution)/shard_map/gather | solution.py:74
  150.1 1.4 convolution_bitcast_fusion.5
  151.7 11.8 %scatter_custom_fusion = f32[128,384]{0,1:T(8,128)S(1)} fusion(s32[2000]{0:T(1024)S(1)} %reshape.228, f32[2000,128]{1,0:T(8,128)S(1)} %reshape.214, f32[]{:T(128)} %constant.45.clone.1), kind=kCustom, calls=%fused_computation.37 | custom fusion | flops 256000 | bytes 196612 | tf_op jit(solution)/shard_map/scatter-add | solution.py:78
  163.5 1.9 convolution_bitcast_fusion.2
  165.4 4.5 %copy.61 = f32[64,128,2,32]{0,3,2,1:T(8,128)} copy(f32[64,128,2,32]{1,0,2,3:T(8,128)S(1)} %convolution_bitcast_fusion.2) | data formatting | bytes 4194304 | tf_op jit(solution)/shard_map/kpr,ckj->pcrj/transpose | solution.py:51
  169.9 6.7 %copy.62 = f32[64,1,8192]{2,1,0:T(1,128)} copy(f32[64,1,8192]{0,2,1:T(8,128)} %bitcast.93) | data formatting | bytes 4194304 | tf_op jit(solution)/shard_map/all_to_all | solution.py:54
  176.7 8.0 %all-to-all-start.1 = ((f32[64,1,8192]{2,1,0:T(1,128)}), f32[64,1,8192]{2,1,0:T(1,128)S(1)}, u32[]{:S(2)}, u32[]{:S(2)}) async-start(f32[64,1,8192]{2,1,0:T(1,128)} %copy.62), calls=%async_computation.1 | async-start | bytes 4194304 | tf_op jit(solution)/shard_map/all_to_all | solution.py:54
  184.7 49.2 %all-to-all-done.1 = f32[64,1,8192]{2,1,0:T(1,128)S(1)} async-done(((f32[64,1,8192]{2,1,0:T(1,128)}), f32[64,1,8192]{2,1,0:T(1,128)S(1)}, u32[]{:S(2)}, u32[]{:S(2)}) %all-to-all-start.1) | async-done | bytes 2097184 | tf_op jit(solution)/shard_map/all_to_all | solution.py:54
  233.9 4.5 %copy.63 = f32[64,1,8192]{0,2,1:T(8,128)} copy(f32[64,1,8192]{2,1,0:T(1,128)S(1)} %all-to-all-done.1) | data formatting | bytes 4194304 | tf_op jit(solution)/shard_map/all_to_all | solution.py:54
  238.3 8.1 %fusion.11 = f32[128,4,32]{0,1,2:T(4,128)S(1)} fusion(f32[64,128,2,32]{0,3,2,1:T(8,128)} %bitcast.98, f32[4,2]{0,1:T(2,128)S(1)} %compare_convert_fusion, f32[4,64]{1,0:T(4,128)S(1)} %fusion.65), kind=kOutput, calls=%fused_computation.23 | convolution fusion | flops 25166336 | bytes 2163744 | tf_op jit(solution)/shard_map/kpr,pcrj->ckj/dot_general | solution.py:61
  246.5 1.3 scatter_fusion
  247.8 0.1 copy.66
  248.1 0.7 gather_fusion.2
  248.7 1.9 convolution_bitcast_fusion.1
  250.6 4.5 %copy.69 = f32[64,128,2,32]{0,3,2,1:T(8,128)} copy(f32[64,128,2,32]{1,0,2,3:T(8,128)S(1)} %convolution_bitcast_fusion.1) | data formatting | bytes 4194304 | tf_op jit(solution)/shard_map/kpr,ckj->pcrj/transpose | solution.py:35
  255.1 5.4 %copy.70 = f32[64,1,8192]{2,1,0:T(1,128)S(1)} copy(f32[64,1,8192]{0,2,1:T(8,128)} %bitcast.94) | data formatting | bytes 4194304 | tf_op jit(solution)/shard_map/all_to_all | solution.py:36
  260.5 56.5 %all_to_all.36 = f32[64,1,8192]{2,1,0:T(1,128)} all-to-all(f32[64,1,8192]{2,1,0:T(1,128)S(1)} %copy.70), channel_id=1, replica_groups=mesh['mesh'=64,'state'=8] {'mesh'}, dimensions={0} | all-to-all | bytes 4194304 | tf_op jit(solution)/shard_map/all_to_all | solution.py:36
  316.9 6.7 %copy.71 = f32[64,1,8192]{0,2,1:T(8,128)} copy(f32[64,1,8192]{2,1,0:T(1,128)} %all_to_all.36) | data formatting | bytes 4194304 | tf_op jit(solution)/shard_map/all_to_all | solution.py:36
  323.6 8.1 %fusion.14 = f32[128,4,32]{0,1,2:T(4,128)S(1)} fusion(f32[64,128,2,32]{0,3,2,1:T(8,128)} %bitcast.99, f32[4,2]{0,1:T(2,128)S(1)} %compare_convert_fusion, f32[4,64]{1,0:T(4,128)S(1)} %fusion.65), kind=kOutput, calls=%fused_computation.24 | convolution fusion | flops 25166336 | bytes 2163744 | tf_op jit(solution)/shard_map/kpr,pcrj->ckj/dot_general | solution.py:43
  331.9 0.1 copy.75
  332.0 5.6 %gather_fusion.3 = f32[2000,128]{1,0:T(8,128)S(1)} fusion(f32[128,384]{0,1:T(8,128)S(1)} %copy.75, s32[2048]{0:T(1024)S(1)} %pad_clamp_fusion), kind=kCustom, calls=%fused_computation.3 | custom fusion | bytes 2056000 | tf_op jit(solution)/shard_map/gather | solution.py:74
  337.7 1.4 convolution_bitcast_fusion.4
  339.2 11.8 %scatter_custom_fusion.2 = f32[128,384]{0,1:T(8,128)S(1)} fusion(s32[2000]{0:T(1024)S(1)} %reshape.228, f32[2000,128]{1,0:T(8,128)S(1)} %reshape.230, f32[]{:T(128)} %constant.45.clone.1), kind=kCustom, calls=%fused_computation.35 | custom fusion | flops 256000 | bytes 196612 | tf_op jit(solution)/shard_map/scatter-add | solution.py:78
  351.1 1.9 convolution_bitcast_fusion
  353.0 4.5 %copy.79 = f32[64,128,2,32]{0,3,2,1:T(8,128)} copy(f32[64,128,2,32]{1,0,2,3:T(8,128)S(1)} %convolution_bitcast_fusion) | data formatting | bytes 4194304 | tf_op jit(solution)/shard_map/kpr,ckj->pcrj/transpose | solution.py:51
  357.5 6.7 %copy.80 = f32[64,1,8192]{2,1,0:T(1,128)} copy(f32[64,1,8192]{0,2,1:T(8,128)} %bitcast.95) | data formatting | bytes 4194304 | tf_op jit(solution)/shard_map/all_to_all | solution.py:54
  364.2 7.7 %all-to-all-start.3 = ((f32[64,1,8192]{2,1,0:T(1,128)}), f32[64,1,8192]{2,1,0:T(1,128)S(1)}, u32[]{:S(2)}, u32[]{:S(2)}) async-start(f32[64,1,8192]{2,1,0:T(1,128)} %copy.80), calls=%async_computation.3 | async-start | bytes 4194304 | tf_op jit(solution)/shard_map/all_to_all | solution.py:54
  372.0 49.0 %all-to-all-done.3 = f32[64,1,8192]{2,1,0:T(1,128)S(1)} async-done(((f32[64,1,8192]{2,1,0:T(1,128)}), f32[64,1,8192]{2,1,0:T(1,128)S(1)}, u32[]{:S(2)}, u32[]{:S(2)}) %all-to-all-start.3) | async-done | bytes 2097184 | tf_op jit(solution)/shard_map/all_to_all | solution.py:54
  421.0 4.5 %copy.81 = f32[64,1,8192]{0,2,1:T(8,128)} copy(f32[64,1,8192]{2,1,0:T(1,128)S(1)} %all-to-all-done.3) | data formatting | bytes 4194304 | tf_op jit(solution)/shard_map/all_to_all | solution.py:54
  425.5 8.2 %fusion.17 = f32[128,4,32]{0,1,2:T(4,128)S(1)} fusion(f32[64,128,2,32]{0,3,2,1:T(8,128)} %bitcast.96, f32[4,2]{0,1:T(2,128)S(1)} %compare_convert_fusion, f32[4,64]{1,0:T(4,128)S(1)} %fusion.65), kind=kOutput, calls=%fused_computation.25 | convolution fusion | flops 25166336 | bytes 2163744 | tf_op jit(solution)/shard_map/kpr,pcrj->ckj/dot_general | solution.py:61
  433.7 1.3 scatter_fusion.1
  435.0 0.1 copy.84
  435.1 0.7 multiply_subtract_fusion
  (49 shorter events, 0.9 us)
Async XLA Ops:
  6.5 48.9 %copy-start = (f32[128,2048]{1,0:T(8,128)S(1)}, f32[128,2048]{1,0:T(8,128)}, u32[]{:S(2)}) copy-start(f32[128,2048]{1,0:T(8,128)} %param.7) | copy-start | bytes 3145732
  6.5 48.9 %all-gather.2.cloned.1.call-start = ((), (), s32[]{:S(2)}) async-start(), calls=%async_computation.4 | async-start | bytes 2359296 | tf_op jit(solution)/shard_map/all_gather | solution.py:17
  65.3 16.8 %copy-start.8 = (s32[16,125]{1,0:T(8,128)S(1)}, s32[16,125]{1,0:T(8,128)}, u32[]{:S(2)}) copy-start(s32[16,125]{1,0:T(8,128)} %param.9) | copy-start | bytes 24004
  72.0 59.5 %all-to-all-start = ((f32[64,1,8192]{2,1,0:T(1,128)}), f32[64,1,8192]{2,1,0:T(1,128)S(1)}, u32[]{:S(2)}, u32[]{:S(2)}) async-start(f32[64,1,8192]{2,1,0:T(1,128)} %copy.52), calls=%async_computation | async-start | bytes 4194304 | tf_op jit(solution)/shard_map/all_to_all | solution.py:36
  144.5 5.7 %copy-start.4 = (f32[16,125,125]{2,0,1:T(8,128)S(1)}, f32[16,125,125]{2,0,1:T(8,128)}, u32[]{:S(2)}) copy-start(f32[16,125,125]{2,0,1:T(8,128)} %param.8) | copy-start | bytes 3000004
  163.5 21.2 %copy-start.3 = (f32[128,384]{0,1:T(8,128)}, f32[128,384]{0,1:T(8,128)S(1)}, u32[]{:S(2)}) copy-start(f32[128,384]{0,1:T(8,128)S(1)} %scatter_custom_fusion) | copy-start | bytes 589828
  176.7 57.2 %all-to-all-start.1 = ((f32[64,1,8192]{2,1,0:T(1,128)}), f32[64,1,8192]{2,1,0:T(1,128)S(1)}, u32[]{:S(2)}, u32[]{:S(2)}) async-start(f32[64,1,8192]{2,1,0:T(1,128)} %copy.62), calls=%async_computation.1 | async-start | bytes 4194304 | tf_op jit(solution)/shard_map/all_to_all | solution.py:54
  184.7 61.8 %slice-start.1 = ((f32[128,384]{0,1:T(8,128)}), f32[128,256]{0,1:T(8,128)S(1)}, s32[]{:S(2)}) async-start(f32[128,384]{0,1:T(8,128)} %copy-done.3), calls=%async_computation.6 | async-start | bytes 262144 | tf_op jit(solution)/shard_map/slice | solution.py:82
  247.9 7.2 %copy-start.6 = (f32[128,256]{1,0:T(8,128)}, f32[128,256]{1,0:T(8,128)S(1)}, u32[]{:S(2)}) copy-start(f32[128,256]{1,0:T(8,128)S(1)} %copy.66) | copy-start | bytes 393220
  332.0 5.7 %copy-start.5 = (f32[16,125,125]{2,0,1:T(8,128)S(1)}, f32[16,125,125]{2,0,1:T(8,128)}, u32[]{:S(2)}) copy-start(f32[16,125,125]{2,0,1:T(8,128)} %param.8) | copy-start | bytes 3000004
  351.1 20.9 %copy-start.2 = (f32[128,384]{0,1:T(8,128)}, f32[128,384]{0,1:T(8,128)S(1)}, u32[]{:S(2)}) copy-start(f32[128,384]{0,1:T(8,128)S(1)} %scatter_custom_fusion.2) | copy-start | bytes 589828
  364.2 56.8 %all-to-all-start.3 = ((f32[64,1,8192]{2,1,0:T(1,128)}), f32[64,1,8192]{2,1,0:T(1,128)S(1)}, u32[]{:S(2)}, u32[]{:S(2)}) async-start(f32[64,1,8192]{2,1,0:T(1,128)} %copy.80), calls=%async_computation.3 | async-start | bytes 4194304 | tf_op jit(solution)/shard_map/all_to_all | solution.py:54
  372.0 61.7 %slice-start = ((f32[128,384]{0,1:T(8,128)}), f32[128,256]{0,1:T(8,128)S(1)}, s32[]{:S(2)}) async-start(f32[128,384]{0,1:T(8,128)} %copy-done.2), calls=%async_computation.5 | async-start | bytes 262144 | tf_op jit(solution)/shard_map/slice | solution.py:82
  421.0 14.8 %copy-start.1 = (f32[128,2048]{1,0:T(8,128)S(1)}, f32[128,2048]{1,0:T(8,128)}, u32[]{:S(2)}) copy-start(f32[128,2048]{1,0:T(8,128)} %param.7) | copy-start | bytes 3145732
  425.5 9.7 %copy-start.7 = (f32[128,256]{1,0:T(8,128)S(1)}, f32[128,256]{1,0:T(8,128)}, u32[]{:S(2)}) copy-start(f32[128,256]{1,0:T(8,128)} %copy-done.6) | copy-start | bytes 393220
Sparse Core Ops, SparseCore 0:
  9.5 45.8 all-gather.1
where the time goes:
time: 449 us; the launch traced here: 443 us
  waiting for transfers between devices  195 us (43%)
  local copies, waits for them, and re-layouts  78.1 us (17%)
  blocking collectives  56.5 us (13%)
  matrix products  45.8 us (10%)
  other arithmetic  27.9 us (6%)
  starting transfers between devices  25.7 us (6%)
  between operations  14.1 us (3%)
    all_to_all x2, waiting for transfers between devices, return_sums(): lax.all_to_all(going_back.reshape(partitions, block_rows * 2 * halo_width...  98.2 us
    all_to_all x1, blocking collectives, fetch_ghosts(): lax.all_to_all(outgoing.reshape(partitions, block_rows * 2 * halo_width),...  56.5 us
    all_to_all x1, waiting for transfers between devices, fetch_ghosts(): lax.all_to_all(outgoing.reshape(partitions, block_rows * 2 * halo_width),...  49.4 us
    all_gather x1, waiting for transfers between devices, per_device(): lax.all_gather(subspace, 'state', axis=0, tiled=True)  46.6 us
    scatter-add x2, other arithmetic, apply_ham(): summed = jnp.zeros(extended.shape, jnp.float32).at[:, connect].add(products)  23.7 us
    all_to_all x4, local copies, waits for them, and re-layouts, fetch_ghosts(): lax.all_to_all(outgoing.reshape(partitions, block_rows * 2 * halo_width),...  23.2 us
    all_to_all x4, local copies, waits for them, and re-layouts, return_sums(): lax.all_to_all(going_back.reshape(partitions, block_rows * 2 * halo_width...  22.4 us
    dot_general x2, matrix products, return_sums(): jnp.einsum('kpr,pcrj->ckj', take_route, arrived.reshape(partitions, block...  16.3 us
  transfers between devices with their start and end apart: 4, of which 4 were waited for; matrix products, arithmetic and copies ran while one was open for 0% of the time, Pallas kernels for 0%

commit v1 on v0

v1 whole, which is shorter than its diff:
```python
import functools

import jax
import jax.numpy as jnp
from jax import lax
from jax.experimental import pallas as pl
from jax.experimental.pallas import tpu as pltpu
from jax.sharding import PartitionSpec as P

MESH = pl.DeviceIdType.MESH
F32 = jnp.float32
BF16 = jnp.bfloat16
PIECES = 4


def split(value):
    high = value.astype(BF16)
    low = (value - high.astype(F32)).astype(BF16)
    return high, low


def dot(left, right):
    return jnp.dot(left, right, preferred_element_type=F32)


def dot_nt(left, right):
    return lax.dot_general(
        left, right, (((1,), (1,)), ((), ())), preferred_element_type=F32
    )


def left3(value):
    high, low = split(value)
    return jnp.concatenate([high, low, high], axis=1)


def right3(value, axis):
    high, low = split(value)
    return jnp.concatenate([high, high, low], axis=axis)


def right2(value, axis):
    high, low = split(value)
    return jnp.concatenate([high, low], axis=axis)


def kernel(
    n_mesh,
    sub_hbm,
    ritz_hbm,
    ham_hbm,
    connect_hbm,
    rows_hbm,
    out_ref,
    gathered,
    ritz_in,
    ritz_cat,
    ham_in,
    ham_pad,
    connect_in,
    connect_pad,
    rows_in,
    op_sum,
    op_cat,
    op_gg,
    op_og,
    start_acc,
    sends,
    takes,
    local_sem,
    ag_send,
    ag_recv,
    halo_send,
    halo_recv,
):
    own_part = lax.axis_index("mesh")
    state = lax.axis_index("state")
    core = lax.rem(state, 2)
    sibling = state + 1 - 2 * core
    right = lax.rem(state + 2, 8)
    left = lax.rem(state + 6, 8)
    across = lax.rem(state + 4, 8)
    above = lax.rem(own_part + 1, n_mesh)
    below = lax.rem(own_part + n_mesh - 1, n_mesh)
    far = lax.rem(own_part + n_mesh // 2, n_mesh)

    barrier = pltpu.get_barrier_semaphore()
    for peer in (sibling, right, left):
        pl.semaphore_signal(
            barrier, inc=1, device_id={"state": peer}, device_id_type=MESH
        )
    for peer in (above, below, far):
        pl.semaphore_signal(
            barrier, inc=1, device_id={"mesh": peer}, device_id_type=MESH
        )

    loads = [
        pltpu.make_async_copy(connect_hbm, connect_in, local_sem.at[0]),
        pltpu.make_async_copy(rows_hbm, rows_in, local_sem.at[1]),
        pltpu.make_async_copy(ham_hbm, ham_in, local_sem.at[2]),
        pltpu.make_async_copy(sub_hbm, gathered.at[state], local_sem.at[3]),
        pltpu.make_async_copy(ritz_hbm, ritz_in, local_sem.at[4]),
    ]
    for load in loads:
        load.start()
    pl.semaphore_wait(barrier, 6)

    n = PIECES
    size = 256 // n
    half = n // 2

    def transfer(source, target, number, peer):
        return pltpu.make_async_remote_copy(
            src_ref=source,
            dst_ref=target,
            send_sem=ag_send.at[number],
            recv_sem=ag_recv.at[number],
            device_id={"state": peer},
            device_id_type=MESH,
        )

    def piece(owner, i):
        return gathered.at[owner, pl.ds(i * size, size)]

    def own_piece(i):
        return sub_hbm.at[pl.ds(i * size, size)]

    def to_right(i, source, owner):
        return transfer(source, piece(owner, i), i, right)

    def to_left(i, source, owner):
        return transfer(source, piece(owner, i), n + i, left)

    def on_right(i, owner):
        return transfer(piece(owner, i), piece(owner, i), 2 * n + i, right)

    def on_left(i, owner):
        return transfer(piece(owner, i), piece(owner, i), 2 * n + i, left)

    def to_sibling(i, base, owner):
        return transfer(
            piece(owner, i), piece(owner, i), (3 + base) * n + i, sibling
        )

    own_sibling = transfer(sub_hbm, gathered.at[state], 6 * n, sibling)
    started = [own_sibling]
    lows = list(range(half))
    highs = list(range(half, n))
    order = list(zip(lows + highs, highs + lows))
    for i, j in order:
        a = to_right(i, own_piece(i), state)
        b = to_left(j, own_piece(j), state)
        a.start()
        b.start()
        started += [a, b]
        if i == 0:
            own_sibling.start()

    loads[0].wait()
    loads[1].wait()
    connect_pad[...] = jnp.full((16, 128), -1, jnp.int32)
    connect_pad[:, 0:125] = connect_in[...]
    ham_pad[...] = jnp.zeros((16, 128, 128), F32)
    loads[2].wait()
    ham_pad[:, 0:125, 0:125] = ham_in[...]
    op_sum[...] = jnp.zeros((384, 384), F32)

    def assemble(e, carry):
        names = connect_pad[pl.ds(e, 1), :]
        names = jnp.where(
            names >= 352, names - 32, jnp.where(names >= 320, names + 32, names)
        )
        pick = (
            lax.broadcasted_iota(jnp.int32, (384, 128), 0) == names
        ).astype(F32).astype(BF16)
        high, low = split(ham_pad[e])
        pick2 = jnp.concatenate([pick, pick], axis=1)
        spread = dot_nt(jnp.concatenate([high, low], axis=1), pick2)
        op_sum[...] += dot(pick2, right2(spread, 0))
        return carry

    lax.fori_loop(0, 16, assemble, 0)

    send_names = jnp.concatenate(
        [rows_in[0, pl.ds(k, 1), :] for k in range(4)], axis=1
    )
    place_f = (
        lax.broadcasted_iota(jnp.int32, (256, 128), 0) == send_names
    ).astype(F32)
    place = place_f.astype(BF16)
    take = jnp.transpose(place_f).astype(BF16)
    take2 = jnp.concatenate([take, take], axis=1)
    place2 = jnp.concatenate([place, place], axis=1)
    same = dot(take, place).astype(BF16)
    same2 = jnp.concatenate([same, same], axis=1)
    take_rows2 = jnp.concatenate([take, take], axis=0)

    centre = 2.5
    eye = (
        lax.broadcasted_iota(jnp.int32, (384, 256), 0)
        == lax.broadcasted_iota(jnp.int32, (384, 256), 1)
    ).astype(F32)
    op_cat[...] = left3(op_sum[:, 0:256] - centre * eye)
    ghost_cols = left3(op_sum[:, 256:384])
    op_og[...] = ghost_cols[0:256]
    op_gg[...] = ghost_cols[256:384]

    loads[4].wait()
    for i in range(16):
        ritz_cat[i] = left3(ritz_in[:, 128 * i : 128 * i + 128])

    def rotate(owner, h):
        block = gathered[owner, 128 * h : 128 * h + 128, :]
        start_acc[...] += dot(ritz_cat[2 * owner + h], right3(block, 0))

    start_acc[...] = jnp.zeros((128, 256), F32)
    loads[3].wait()
    rotate(state, 0)
    rotate(state, 1)

    def pass_on(copies):
        for copy in copies:
            copy.start()
        started.extend(copies)

    for i, j in zip(lows, highs):
        to_right(i, piece(left, i), left).wait_recv()
        pass_on([on_right(i, left), to_sibling(i, 0, left)])
        to_left(j, piece(right, j), right).wait_recv()
        pass_on([on_left(j, right), to_sibling(j, 1, right)])
    transfer(gathered.at[sibling], gathered.at[sibling], 6 * n, sibling).wait_recv()
    rotate(sibling, 0)
    rotate(sibling, 1)
    rotate(left, 0)
    rotate(right, 1)
    for i, j in zip(highs, lows):
        to_right(i, piece(left, i), left).wait_recv()
        pass_on([to_sibling(i, 0, left)])
        to_left(j, piece(right, j), right).wait_recv()
        pass_on([to_sibling(j, 1, right)])
    rotate(left, 1)
    rotate(right, 0)
    other_left = lax.rem(sibling + 6, 8)
    other_right = lax.rem(sibling + 2, 8)
    other_across = lax.rem(sibling + 4, 8)
    for i, j in zip(lows, highs):
        on_right(i, across).wait_recv()
        pass_on([to_sibling(i, 2, across)])
        on_left(j, across).wait_recv()
        pass_on([to_sibling(j, 2, across)])
    for h, pieces in ((0, lows), (1, highs)):
        for i in pieces:
            to_sibling(i, 0, other_left).wait_recv()
        rotate(other_left, h)
        for i in pieces:
            to_sibling(i, 1, other_right).wait_recv()
        rotate(other_right, h)
    rotate(across, 0)
    rotate(across, 1)
    for h, pieces in ((0, lows), (1, highs)):
        for i in pieces:
            to_sibling(i, 2, other_across).wait_recv()
        rotate(other_across, h)

    start = start_acc[...]

    def exchange(number):
        copies = []
        for k, (first, count, target, peer) in enumerate(
            ((0, 32, 32, above), (32, 32, 0, below), (64, 64, 64, far))
        ):
            copies.append(
                pltpu.make_async_remote_copy(
                    src_ref=sends.at[number, pl.ds(first, count)],
                    dst_ref=takes.at[number, pl.ds(target, count)],
                    send_sem=halo_send.at[number, k],
                    recv_sem=halo_recv.at[number, k],
                    device_id={"mesh": peer},
                    device_id_type=MESH,
                )
            )
        for copy in copies:
            copy.start()
        started.extend(copies)
        return copies

    def arrive(copies):
        for copy in copies:
            copy.wait_recv()
        return takes[len(halos) - 1]

    sigma_one = 1.5 / (-1.0 - centre)
    sigma_two = 1.0 / (2.0 / sigma_one - sigma_one)
    scale_one = sigma_one / 1.5
    scale_two = 2.0 * sigma_two / 1.5
    halos = []

    sends[0] = dot_nt(take2, right2(start, 1))
    halos.append(exchange(0))
    base = dot_nt(op_cat[...], right3(start, 1))
    ghosts = right3(arrive(halos[0]), 0)
    sends[1] = base[256:384] + dot(op_gg[...], ghosts)
    halos.append(exchange(1))
    own = base[0:256] + dot(op_og[...], ghosts)
    own_packed = dot(take2, right2(own, 0))
    back = right2(arrive(halos[1]), 0)
    sends[2] = scale_one * (own_packed + dot(same2, back))
    halos.append(exchange(2))
    first = scale_one * (own + dot(place2, back))
    base = dot(op_cat[...], right3(first, 0))
    ghosts = right3(arrive(halos[2]), 0)
    sends[3] = base[256:384] + dot(op_gg[...], ghosts)
    halos.append(exchange(3))
    own = base[0:256] + dot(op_og[...], ghosts)
    rest = scale_two * jnp.transpose(own) - sigma_one * sigma_two * start
    back = right2(jnp.transpose(arrive(halos[3])), 1)
    out_ref[...] = rest + scale_two * dot(back, take_rows2)

    for copy in started:
        copy.wait_send()


def solution(mesh):
    n_mesh = mesh.shape["mesh"]

    def per_device(subspace, ritz, element_ham, connect, send_rows):
        any_space = pl.BlockSpec(memory_space=pl.ANY)
        copies = 6 * PIECES + 1
        return pl.pallas_call(
            functools.partial(kernel, n_mesh),
            out_shape=jax.ShapeDtypeStruct((128, 256), F32),
            in_specs=[any_space] * 5,
            out_specs=pl.BlockSpec(memory_space=pltpu.VMEM),
            scratch_shapes=[
                pltpu.VMEM((8, 256, 256), F32),
                pltpu.VMEM((128, 2048), F32),
                pltpu.VMEM((16, 128, 384), BF16),
                pltpu.VMEM((16, 125, 125), F32),
                pltpu.VMEM((16, 128, 128), F32),
                pltpu.VMEM((16, 125), jnp.int32),
                pltpu.VMEM((16, 128), jnp.int32),
                pltpu.VMEM((1, 4, 32), jnp.int32),
                pltpu.VMEM((384, 384), F32),
                pltpu.VMEM((384, 768), BF16),
                pltpu.VMEM((128, 384), BF16),
                pltpu.VMEM((256, 384), BF16),
                pltpu.VMEM((128, 256), F32),
                pltpu.VMEM((4, 128, 128), F32),
                pltpu.VMEM((4, 128, 128), F32),
                pltpu.SemaphoreType.DMA((5,)),
                pltpu.SemaphoreType.DMA((copies,)),
                pltpu.SemaphoreType.DMA((copies,)),
                pltpu.SemaphoreType.DMA((4, 3)),
                pltpu.SemaphoreType.DMA((4, 3)),
            ],
            compiler_params=pltpu.CompilerParams(
                collective_id=0,
                has_side_effects=True,
                vmem_limit_bytes=40 * 1024 * 1024,
            ),
        )(subspace, ritz, element_ham, connect, send_rows)

    return jax.shard_map(
        per_device,
        mesh=mesh,
        in_specs=(
            P("state", "mesh"),
            P("state", None),
            P("mesh", None, None),
            P("mesh", None),
            P("mesh", None, None),
        ),
        out_specs=P("state", "mesh"),
        check_vma=False,
    )
```

time: 449 us -> 54.4 us (0.12); the launches traced: 443 us -> 53.8 us
  waiting for transfers between devices: 195 us -> 0 us
  local copies, waits for them, and re-layouts: 78.1 us -> 2.33 us
  blocking collectives: 56.5 us -> 0 us
  Pallas kernels: 0 us -> 51.4 us
  matrix products: 45.8 us -> 0 us
  other arithmetic: 27.9 us -> 0 us
  starting transfers between devices: 25.7 us -> 0 us
  between operations: 14.1 us -> 0.06 us
    all_to_all x3 -> x0, waiting for transfers between devices: 148 us -> none  [the longest x2 98.2 us: return_sums(): lax.all_to_all(going_back.reshape(partitions, block_rows * 2 * halo_width...]
    all_to_all x1 -> x0, blocking collectives: 56.5 us -> none  [fetch_ghosts(): lax.all_to_all(outgoing.reshape(partitions, block_rows * 2 * halo_width),...]
    pallas_call x0 -> x1, Pallas kernels: none -> 51.4 us  [per_device(): pl.pallas_call(functools.partial(kernel, n_mesh), out_shape=jax.ShapeDtyp...]
    all_gather x1 -> x0, waiting for transfers between devices: 46.6 us -> none  [per_device(): lax.all_gather(subspace, 'state', axis=0, tiled=True)]
    dot_general x11 -> x0, matrix products: 45.8 us -> none  [the longest x2 16.3 us: return_sums(): jnp.einsum('kpr,pcrj->ckj', take_route, arrived.reshape(partitions, block...]
    all_to_all x8 -> x0, local copies, waits for them, and re-layouts: 45.6 us -> none  [the longest x4 23.2 us: fetch_ghosts(): lax.all_to_all(outgoing.reshape(partitions, block_rows * 2 * halo_width),...]
    scatter-add x4 -> x0, other arithmetic: 26.3 us -> none  [the longest x2 23.7 us: apply_ham(): summed = jnp.zeros(extended.shape, jnp.float32).at[:, connect].add(products)]
    all_to_all x3 -> x0, starting transfers between devices: 25.7 us -> none  [the longest x2 15.7 us: return_sums(): lax.all_to_all(going_back.reshape(partitions, block_rows * 2 * halo_width...]
  transfers between devices with their start and end apart: 4 -> 0, of which waited for: 4 -> 0; matrix products, arithmetic and copies ran while one was open for 0% -> 0% of each run, Pallas kernels for 0% -> 0%
where the time goes in v1:
time: 54.4 us; the launch traced here: 53.8 us
  Pallas kernels  51.4 us (94%)
  local copies, waits for them, and re-layouts  2.33 us (4%)
    pallas_call x1, Pallas kernels, per_device(): pl.pallas_call(functools.partial(kernel, n_mesh), out_shape=jax.ShapeDtyp...  51.4 us
    unnamed x10, local copies, waits for them, and re-layouts  2.33 us

profile of v1, /device:TPU:1, one launch (start us, length us, event | category | flops | bytes accessed | tf_op | source)
XLA Modules:
  0.0 53.8 jit_solution(12968922724113805253)
XLA Ops:
  0.0 0.0 copy-start.3
  0.0 0.0 copy-start.2
  0.0 0.0 copy-start
  0.0 0.0 copy-start.1
  0.0 1.7 %copy.6.ham_hbm = f32[16,125,125]{2,1,0:T(8,128)S(1)} copy(f32[16,125,125]{2,0,1:T(8,128)} %param.7) | data formatting | bytes 2000000 | tf_op args[2]
  1.7 0.0 copy-done.3
  1.7 0.0 copy-done.2
  1.7 0.0 copy-done
  1.7 0.0 copy-done.1
  1.7 51.4 %shard_map.55 = f32[128,256]{1,0:T(8,128)S(1)} custom-call(f32[256,256]{1,0:T(8,128)S(1)} %copy-done.1, f32[128,2048]{1,0:T(8,128)S(1)} %copy-done, f32[16,125,125]{2,1,0:T(8,128)S(1)} %copy.6.ham_hbm, s32[16,125]{1,0:T(8,128)S(1)} %copy-done.2, s32[1,4,32]{2,1,0:T(4,128)S(1)} %copy-done.3), custom_call_target="tpu_custom_call" | custom-call | tf_op jit(solution)/shard_map/pallas_call | solution.py:329
  53.1 0.7 %copy.8 = f32[128,256]{1,0:T(8,128)} copy(f32[128,256]{1,0:T(8,128)S(1)} %shard_map.55) | data formatting | bytes 262144
Async XLA Ops:
  0.0 1.7 %copy-start.3 = (s32[1,4,32]{2,1,0:T(4,128)S(1)}, s32[1,4,32]{2,1,0:T(4,128)}, u32[]{:S(2)}) copy-start(s32[1,4,32]{2,1,0:T(4,128)} %rows_hbm.1) | copy-start | bytes 1540
  0.0 1.7 %copy-start.2 = (s32[16,125]{1,0:T(8,128)S(1)}, s32[16,125]{1,0:T(8,128)}, u32[]{:S(2)}) copy-start(s32[16,125]{1,0:T(8,128)} %connect_hbm.1) | copy-start | bytes 24004
  0.0 1.7 %copy-start = (f32[128,2048]{1,0:T(8,128)S(1)}, f32[128,2048]{1,0:T(8,128)}, u32[]{:S(2)}) copy-start(f32[128,2048]{1,0:T(8,128)} %ritz_hbm.1) | copy-start | bytes 3145732
  0.0 1.7 %copy-start.1 = (f32[256,256]{1,0:T(8,128)S(1)}, f32[256,256]{1,0:T(8,128)}, u32[]{:S(2)}) copy-start(f32[256,256]{1,0:T(8,128)} %sub_hbm.1) | copy-start | bytes 786436

commit v2 on v1

v2 whole, which is shorter than its diff:
```python
import functools

import jax
import jax.numpy as jnp
from jax import lax
from jax.experimental import pallas as pl
from jax.experimental.pallas import tpu as pltpu
from jax.sharding import PartitionSpec as P

MESH = pl.DeviceIdType.MESH
F32 = jnp.float32
BF16 = jnp.bfloat16
PIECES = 8
SIDE = PIECES // 2
SIZE = 256 // PIECES


def split(value):
    high = value.astype(BF16)
    low = (value - high.astype(F32)).astype(BF16)
    return high, low


def dot(left, right):
    return jnp.dot(left, right, preferred_element_type=F32)


def dot_nt(left, right):
    return lax.dot_general(
        left, right, (((1,), (1,)), ((), ())), preferred_element_type=F32
    )


def left3(value):
    high, low = split(value)
    return jnp.concatenate([high, low, high], axis=1)


def right3(value, axis):
    high, low = split(value)
    return jnp.concatenate([high, high, low], axis=axis)


def right2(value, axis):
    high, low = split(value)
    return jnp.concatenate([high, low], axis=axis)


def kernel(
    n_mesh,
    sub_hbm,
    ritz_hbm,
    ham_hbm,
    connect_hbm,
    rows_hbm,
    out_ref,
    gathered,
    ritz_in,
    ritz_cat,
    ham_in,
    ham_pad,
    connect_in,
    connect_pad,
    rows_in,
    op_sum,
    op_cat,
    op_gg,
    op_og,
    start_acc,
    sends,
    takes,
    local_sem,
    ready,
    own_send,
    own_recv,
    on_send,
    on_recv,
    core_send,
    core_recv,
    halo_send,
    halo_recv,
):
    own_part = lax.axis_index("mesh")
    state = lax.axis_index("state")
    core = lax.rem(state, 2)
    flip = 1 - 2 * core
    sibling = state + flip
    height = lax.div(state, 2)
    across = lax.rem(state + 4, 8)
    above = lax.rem(own_part + 1, n_mesh)
    below = lax.rem(own_part + n_mesh - 1, n_mesh)
    far = lax.rem(own_part + n_mesh // 2, n_mesh)

    def towards(d):
        return lax.rem(state + 2 + 4 * d, 8)

    barrier = pltpu.get_barrier_semaphore()

    def tell(peer):
        pl.semaphore_signal(barrier, inc=1, device_id=peer, device_id_type=MESH)

    def answer(slot, peer):
        pl.semaphore_signal(
            ready.at[slot], inc=1, device_id=peer, device_id_type=MESH
        )

    first_height = height == 0
    last_height = height == 3
    last_part = own_part == n_mesh - 1
    first_part = own_part == 0
    upper_half = own_part >= n_mesh // 2
    tell({"state": sibling})
    pl.when(jnp.logical_not(last_height))(lambda: tell({"state": towards(0)}))
    pl.when(first_height)(lambda: tell({"state": towards(1)}))
    pl.when(jnp.logical_not(last_part))(lambda: tell({"mesh": above}))
    pl.when(first_part)(lambda: tell({"mesh": below}))
    pl.when(jnp.logical_not(upper_half))(lambda: tell({"mesh": far}))

    loads = [
        pltpu.make_async_copy(connect_hbm, connect_in, local_sem.at[0]),
        pltpu.make_async_copy(rows_hbm, rows_in, local_sem.at[1]),
        pltpu.make_async_copy(ham_hbm, ham_in, local_sem.at[2]),
        pltpu.make_async_copy(sub_hbm, gathered.at[state], local_sem.at[3]),
        pltpu.make_async_copy(ritz_hbm, ritz_in, local_sem.at[4]),
    ]
    for load in loads:
        load.start()
    told = (
        1
        + jnp.minimum(height, 1)
        + lax.div(height, 3)
        + jnp.minimum(own_part, 1)
        + lax.div(own_part, n_mesh - 1)
        + lax.div(own_part, n_mesh // 2)
    )
    pl.semaphore_wait(barrier, told)
    pl.when(jnp.logical_not(first_height))(lambda: answer(0, {"state": towards(1)}))
    pl.when(last_height)(lambda: answer(1, {"state": towards(0)}))
    pl.when(jnp.logical_not(first_part))(lambda: answer(2, {"mesh": below}))
    pl.when(last_part)(lambda: answer(3, {"mesh": above}))
    pl.when(upper_half)(lambda: answer(4, {"mesh": far}))

    def answered(slot):
        return lambda: pl.semaphore_wait(ready.at[slot], 1)

    def span(i):
        return pl.ds(pl.multiple_of(i * SIZE, SIZE), SIZE)

    def remote(source, target, send_sem, recv_sem, peer):
        return pltpu.make_async_remote_copy(
            src_ref=source,
            dst_ref=target,
            send_sem=send_sem,
            recv_sem=recv_sem,
            device_id={"state": peer},
            device_id_type=MESH,
        )

    def own_copy(d, i, owner):
        return remote(
            sub_hbm.at[span(i)],
            gathered.at[owner, span(i)],
            own_send.at[d, i],
            own_recv.at[d, i],
            towards(d),
        )

    def on_copy(d, i, owner):
        return remote(
            gathered.at[owner, span(i)],
            gathered.at[owner, span(i)],
            on_send.at[d, i],
            on_recv.at[d, i],
            towards(d),
        )

    def core_copy(kind, i, owner):
        return remote(
            gathered.at[owner, span(i)],
            gathered.at[owner, span(i)],
            core_send.at[kind, i],
            core_recv.at[kind, i],
            sibling,
        )

    own_sibling = remote(
        sub_hbm, gathered.at[state], core_send.at[3, 0], core_recv.at[3, 0], sibling
    )
    started = []

    def start(*copies):
        for copy in copies:
            copy.start()
        started.extend(copies)

    a = jnp.minimum(height, 1)
    b = 1 - a

    def first_half(d):
        return [own_copy(d, SIDE * d + i, state) for i in range(SIDE)]

    def second_half(d):
        return [own_copy(d, SIDE * (1 - d) + i, state) for i in range(SIDE)]

    lead, late = second_half(a), second_half(b)

    def start_lead():
        for copy in lead:
            copy.start()

    pl.when(first_height)(answered(0))
    start(*first_half(a))
    pl.when(first_height)(start_lead)
    start(own_sibling)
    pl.when(first_height)(answered(1))
    pl.when(jnp.logical_and(height > 0, height < 3))(answered(0))
    start(*first_half(b))

    loads[0].wait()
    loads[1].wait()
    connect_pad[...] = jnp.full((16, 128), -1, jnp.int32)
    connect_pad[:, 0:125] = connect_in[...]
    ham_pad[...] = jnp.zeros((16, 128, 128), F32)
    loads[2].wait()
    for e in range(16):
        ham_pad[e, 0:125, 0:125] = ham_in[:, e, :]
    op_sum[...] = jnp.zeros((384, 384), F32)

    def assemble(e, carry):
        names = connect_pad[pl.ds(e, 1), :]
        names = jnp.where(
            names >= 352, names - 32, jnp.where(names >= 320, names + 32, names)
        )
        pick = (
            lax.broadcasted_iota(jnp.int32, (384, 128), 0) == names
        ).astype(F32).astype(BF16)
        high, low = split(ham_pad[e])
        pick2 = jnp.concatenate([pick, pick], axis=1)
        spread = dot_nt(jnp.concatenate([high, low], axis=1), pick2)
        op_sum[...] += dot(pick2, right2(spread, 0))
        return carry

    lax.fori_loop(0, 3, assemble, 0)
    pl.when(jnp.logical_not(first_height))(start_lead)
    started.extend(lead)
    start(*late)
    lax.fori_loop(3, 6, assemble, 0)

    send_names = jnp.concatenate(
        [rows_in[0, pl.ds(k, 1), :] for k in range(4)], axis=1
    )
    place_f = (
        lax.broadcasted_iota(jnp.int32, (256, 128), 0) == send_names
    ).astype(F32)
    place = place_f.astype(BF16)
    take = jnp.transpose(place_f).astype(BF16)
    take2 = jnp.concatenate([take, take], axis=1)
    place2 = jnp.concatenate([place, place], axis=1)
    same = dot(take, place).astype(BF16)
    same2 = jnp.concatenate([same, same], axis=1)
    take_rows2 = jnp.concatenate([take, take], axis=0)

    loads[4].wait()
    for i in range(16):
        ritz_cat[i] = left3(ritz_in[:, 128 * i : 128 * i + 128])

    def rotate(owner, h):
        rows = gathered[owner, pl.ds(pl.multiple_of(128 * h, 128), 128), :]
        start_acc[...] += dot(ritz_cat[2 * owner + h], right3(rows, 0))

    start_acc[...] = jnp.zeros((128, 256), F32)
    loads[3].wait()
    rotate(state, 0)
    rotate(state, 1)

    from_a, from_b = towards(a), towards(b)
    for i in range(SIDE):
        for d, owner in ((b, from_a), (a, from_b)):
            k = SIDE * d + i
            own_copy(d, k, owner).wait_recv()
            start(on_copy(d, k, owner), core_copy(d, k, owner))
        lax.fori_loop(6 + 2 * i, 8 + 2 * i, assemble, 0)
    own_sibling.wait_recv()
    rotate(sibling, 0)
    rotate(sibling, 1)
    rotate(from_a, b)
    rotate(from_b, a)
    lax.fori_loop(6 + 2 * SIDE, 16, assemble, 0)
    for i in range(SIDE):
        for d, owner in ((b, from_a), (a, from_b)):
            k = SIDE * (1 - d) + i
            own_copy(d, k, owner).wait_recv()
            start(core_copy(d, k, owner))
    rotate(from_a, a)
    rotate(from_b, b)
    for d, owner in ((b, from_a), (a, from_b)):
        for i in range(SIDE):
            core_copy(d, SIDE * d + i, owner + flip).wait_recv()
        rotate(owner + flip, d)
    centre = 2.5
    eye = (
        lax.broadcasted_iota(jnp.int32, (384, 256), 0)
        == lax.broadcasted_iota(jnp.int32, (384, 256), 1)
    ).astype(F32)
    op_cat[...] = left3(op_sum[:, 0:256] - centre * eye)
    ghost_cols = left3(op_sum[:, 256:384])
    op_og[...] = ghost_cols[0:256]
    op_gg[...] = ghost_cols[256:384]

    for d, owner in ((b, from_a), (a, from_b)):
        for i in range(SIDE):
            core_copy(d, SIDE * (1 - d) + i, owner + flip).wait_recv()
        rotate(owner + flip, 1 - d)
    for i in range(SIDE):
        for d in (b, a):
            k = SIDE * d + i
            on_copy(d, k, across).wait_recv()
            start(core_copy(2, k, across))
    pl.when(jnp.logical_not(last_part))(answered(2))
    pl.when(first_part)(answered(3))
    pl.when(jnp.logical_not(upper_half))(answered(4))
    rotate(across, 0)
    rotate(across, 1)
    for h in range(2):
        for i in range(SIDE):
            core_copy(2, SIDE * h + i, across + flip).wait_recv()
        rotate(across + flip, h)

    block = start_acc[...]

    def exchange(number):
        copies = []
        for k, (first, count, target, peer) in enumerate(
            ((0, 32, 32, above), (32, 32, 0, below), (64, 64, 64, far))
        ):
            copies.append(
                pltpu.make_async_remote_copy(
                    src_ref=sends.at[number, pl.ds(first, count)],
                    dst_ref=takes.at[number, pl.ds(target, count)],
                    send_sem=halo_send.at[number, k],
                    recv_sem=halo_recv.at[number, k],
                    device_id={"mesh": peer},
                    device_id_type=MESH,
                )
            )
        start(*copies)
        return copies

    def arrive(copies):
        for copy in copies:
            copy.wait_recv()
        return takes[len(halos) - 1]

    sigma_one = 1.5 / (-1.0 - centre)
    sigma_two = 1.0 / (2.0 / sigma_one - sigma_one)
    scale_one = sigma_one / 1.5
    scale_two = 2.0 * sigma_two / 1.5
    halos = []

    sends[0] = dot_nt(take2, right2(block, 1))
    halos.append(exchange(0))
    base = dot_nt(op_cat[...], right3(block, 1))
    ghosts = right3(arrive(halos[0]), 0)
    sends[1] = base[256:384] + dot(op_gg[...], ghosts)
    halos.append(exchange(1))
    own = base[0:256] + dot(op_og[...], ghosts)
    own_packed = dot(take2, right2(own, 0))
    back = right2(arrive(halos[1]), 0)
    sends[2] = scale_one * (own_packed + dot(same2, back))
    halos.append(exchange(2))
    first = scale_one * (own + dot(place2, back))
    base = dot(op_cat[...], right3(first, 0))
    ghosts = right3(arrive(halos[2]), 0)
    sends[3] = base[256:384] + dot(op_gg[...], ghosts)
    halos.append(exchange(3))
    own = base[0:256] + dot(op_og[...], ghosts)
    rest = scale_two * jnp.transpose(own) - sigma_one * sigma_two * block
    back = right2(jnp.transpose(arrive(halos[3])), 1)
    out_ref[...] = rest + scale_two * dot(back, take_rows2)

    for copy in started:
        copy.wait_send()


def solution(mesh):
    n_mesh = mesh.shape["mesh"]

    def per_device(subspace, ritz, element_ham, connect, send_rows):
        any_space = pl.BlockSpec(memory_space=pl.ANY)
        hams = jnp.transpose(element_ham, (1, 0, 2))
        return pl.pallas_call(
            functools.partial(kernel, n_mesh),
            out_shape=jax.ShapeDtypeStruct((128, 256), F32),
            in_specs=[any_space] * 5,
            out_specs=pl.BlockSpec(memory_space=pltpu.VMEM),
            scratch_shapes=[
                pltpu.VMEM((8, 256, 256), F32),
                pltpu.VMEM((128, 2048), F32),
                pltpu.VMEM((16, 128, 384), BF16),
                pltpu.VMEM((125, 16, 125), F32),
                pltpu.VMEM((16, 128, 128), F32),
                pltpu.VMEM((16, 125), jnp.int32),
                pltpu.VMEM((16, 128), jnp.int32),
                pltpu.VMEM((1, 4, 32), jnp.int32),
                pltpu.VMEM((384, 384), F32),
                pltpu.VMEM((384, 768), BF16),
                pltpu.VMEM((128, 384), BF16),
                pltpu.VMEM((256, 384), BF16),
                pltpu.VMEM((128, 256), F32),
                pltpu.VMEM((4, 128, 128), F32),
                pltpu.VMEM((4, 128, 128), F32),
                pltpu.SemaphoreType.DMA((5,)),
                pltpu.SemaphoreType.REGULAR((5,)),
                pltpu.SemaphoreType.DMA((2, PIECES)),
                pltpu.SemaphoreType.DMA((2, PIECES)),
                pltpu.SemaphoreType.DMA((2, PIECES)),
                pltpu.SemaphoreType.DMA((2, PIECES)),
                pltpu.SemaphoreType.DMA((4, PIECES)),
                pltpu.SemaphoreType.DMA((4, PIECES)),
                pltpu.SemaphoreType.DMA((4, 3)),
                pltpu.SemaphoreType.DMA((4, 3)),
            ],
            compiler_params=pltpu.CompilerParams(
                collective_id=0,
                has_side_effects=True,
                vmem_limit_bytes=60 * 1024 * 1024,
            ),
        )(subspace, ritz, hams, connect, send_rows)

    return jax.shard_map(
        per_device,
        mesh=mesh,
        in_specs=(
            P("state", "mesh"),
            P("state", None),
            P("mesh", None, None),
            P("mesh", None),
            P("mesh", None, None),
        ),
        out_specs=P("state", "mesh"),
        check_vma=False,
    )
```

time: 54.4 us -> 53.8 us (0.989)
  local copies, waits for them, and re-layouts: 2.33 us -> 1.57 us
  Pallas kernels: 51.4 us -> 52.1 us
    unnamed x10 -> x1, local copies, waits for them, and re-layouts: 2.33 us -> 1.57 us
    pallas_call x1, Pallas kernels: 51.4 us -> 52.1 us  [per_device(): pl.pallas_call(functools.partial(kernel, n_mesh), out_shape=jax.ShapeDtyp...]
where the time goes in v2:
time: 53.8 us; the launch traced here: 53.7 us
  Pallas kernels  52.1 us (97%)
  local copies, waits for them, and re-layouts  1.57 us (3%)
    pallas_call x1, Pallas kernels, per_device(): pl.pallas_call(functools.partial(kernel, n_mesh), out_shape=jax.ShapeDtyp...  52.1 us
    unnamed x1, local copies, waits for them, and re-layouts  1.57 us

profile of v2, /device:TPU:1, one launch (start us, length us, event | category | flops | bytes accessed | tf_op | source)
XLA Modules:
  0.0 53.7 jit_solution(17414663269174479026)
XLA Ops:
  0.0 52.1 %shard_map.55 = f32[128,256]{1,0:T(8,128)} custom-call(f32[256,256]{1,0:T(8,128)} %sub_hbm.1, f32[128,2048]{1,0:T(8,128)} %ritz_hbm.1, f32[125,16,125]{2,1,0:T(8,128)} %bitcast.1, s32[16,125]{1,0:T(8,128)} %connect_hbm.1, s32[1,4,32]{2,1,0:T(4,128)} %rows_hbm.1), custom_call_target="tpu_custom_call" | custom-call | tf_op jit(solution)/shard_map/pallas_call | solution.py:391
  52.1 1.6 %copy.7 = f32[128,256]{1,0:T(8,128)} copy(f32[128,256]{1,0:T(8,128)} %shard_map.55) | data formatting | bytes 262144

commit v3 on v2

--- a/solution.py
+++ b/solution.py
@@ -10,7 +10,7 @@
 MESH = pl.DeviceIdType.MESH
 F32 = jnp.float32
 BF16 = jnp.bfloat16
-PIECES = 8
+PIECES = 4
 SIDE = PIECES // 2
 SIZE = 256 // PIECES
 
@@ -279,13 +279,13 @@
             k = SIDE * d + i
             own_copy(d, k, owner).wait_recv()
             start(on_copy(d, k, owner), core_copy(d, k, owner))
-        lax.fori_loop(6 + 2 * i, 8 + 2 * i, assemble, 0)
+        lax.fori_loop(6 + 8 * i // SIDE, 6 + 8 * (i + 1) // SIDE, assemble, 0)
     own_sibling.wait_recv()
     rotate(sibling, 0)
     rotate(sibling, 1)
     rotate(from_a, b)
     rotate(from_b, a)
-    lax.fori_loop(6 + 2 * SIDE, 16, assemble, 0)
+    lax.fori_loop(14, 16, assemble, 0)
     for i in range(SIDE):
         for d, owner in ((b, from_a), (a, from_b)):
             k = SIDE * (1 - d) + i
@@ -331,7 +331,7 @@
     def exchange(number):
         copies = []
         for k, (first, count, target, peer) in enumerate(
-            ((0, 32, 32, above), (32, 32, 0, below), (64, 64, 64, far))
+            ((64, 64, 64, far), (0, 32, 32, above), (32, 32, 0, below))
         ):
             copies.append(
                 pltpu.make_async_remote_copy(
@@ -390,7 +390,7 @@
         hams = jnp.transpose(element_ham, (1, 0, 2))
         return pl.pallas_call(
             functools.partial(kernel, n_mesh),
-            out_shape=jax.ShapeDtypeStruct((128, 256), F32),
+            out_shape=pltpu.VMEM((128, 256), F32),
             in_specs=[any_space] * 5,
             out_specs=pl.BlockSpec(memory_space=pltpu.VMEM),
             scratch_shapes=[

time: 53.8 us -> 51.9 us (0.965)
  Pallas kernels: 52.1 us -> 51.1 us
  local copies, waits for them, and re-layouts: 1.57 us -> 0.66 us
    pallas_call x1, Pallas kernels: 52.1 us -> 51.1 us  [per_device(): pl.pallas_call(functools.partial(kernel, n_mesh), out_shape=pltpu.VMEM((1...]
    unnamed x1, local copies, waits for them, and re-layouts: 1.57 us -> 0.66 us
where the time goes in v3:
time: 51.9 us; the launch traced here: 51.7 us
  Pallas kernels  51.1 us (98%)
  local copies, waits for them, and re-layouts  0.66 us (1%)
    pallas_call x1, Pallas kernels, per_device(): pl.pallas_call(functools.partial(kernel, n_mesh), out_shape=pltpu.VMEM((1...  51.1 us

profile of v3, /device:TPU:1, one launch (start us, length us, event | category | flops | bytes accessed | tf_op | source)
XLA Modules:
  0.0 51.7 jit_solution(11051585020968916823)
XLA Ops:
  0.0 51.1 %shard_map.55 = f32[128,256]{1,0:T(8,128)S(1)} custom-call(f32[256,256]{1,0:T(8,128)} %sub_hbm.1, f32[128,2048]{1,0:T(8,128)} %ritz_hbm.1, f32[125,16,125]{2,1,0:T(8,128)} %bitcast.1, s32[16,125]{1,0:T(8,128)} %connect_hbm.1, s32[1,4,32]{2,1,0:T(4,128)} %rows_hbm.1), custom_call_target="tpu_custom_call" | custom-call | tf_op jit(solution)/shard_map/pallas_call | solution.py:391
  51.1 0.7 %copy.7 = f32[128,256]{1,0:T(8,128)} copy(f32[128,256]{1,0:T(8,128)S(1)} %shard_map.55) | data formatting | bytes 262144

commit v4 on v3

v4 whole, which is shorter than its diff:
```python
import functools

import jax
import jax.numpy as jnp
from jax import lax
from jax.experimental import pallas as pl
from jax.experimental.pallas import tpu as pltpu
from jax.sharding import PartitionSpec as P

MESH = pl.DeviceIdType.MESH
F32 = jnp.float32
BF16 = jnp.bfloat16
SIZE = 64
GROUP = 4


def split(value):
    high = value.astype(BF16)
    low = (value - high.astype(F32)).astype(BF16)
    return high, low


def dot(left, right):
    return jnp.dot(left, right, preferred_element_type=F32)


def dot_nt(left, right):
    return lax.dot_general(
        left, right, (((1,), (1,)), ((), ())), preferred_element_type=F32
    )


def left3(value):
    high, low = split(value)
    return jnp.concatenate([high, low, high], axis=1)


def right3(value, axis):
    high, low = split(value)
    return jnp.concatenate([high, high, low], axis=axis)


def right2(value, axis):
    high, low = split(value)
    return jnp.concatenate([high, low], axis=axis)


def kernel(
    n_mesh,
    sub_hbm,
    ritz_hbm,
    ham_hbm,
    connect_hbm,
    rows_hbm,
    out_ref,
    gathered,
    ritz_in,
    ritz_cat,
    ham_in,
    ham_pad,
    connect_in,
    connect_pad,
    rows_in,
    op_sum,
    op_cat,
    op_gg,
    op_og,
    same2,
    raw_part,
    start_acc,
    out_acc,
    sends,
    takes,
    local_sem,
    ready,
    own_send,
    own_recv,
    on_send,
    on_recv,
    core_send,
    core_recv,
    halo_send,
    halo_recv,
):
    own_part = lax.axis_index("mesh")
    state = lax.axis_index("state")
    core = lax.rem(state, 2)
    flip = 1 - 2 * core
    sibling = state + flip
    height = lax.div(state, 2)
    across = lax.rem(state + 4, 8)
    above = lax.rem(own_part + 1, n_mesh)
    below = lax.rem(own_part + n_mesh - 1, n_mesh)
    far = lax.rem(own_part + n_mesh // 2, n_mesh)

    def towards(d):
        return lax.rem(state + 2 + 4 * d, 8)

    barrier = pltpu.get_barrier_semaphore()

    def tell(peer):
        pl.semaphore_signal(barrier, inc=1, device_id=peer, device_id_type=MESH)

    def answer(slot, peer):
        pl.semaphore_signal(
            ready.at[slot], inc=1, device_id=peer, device_id_type=MESH
        )

    first_height = height == 0
    last_height = height == 3
    last_part = own_part == n_mesh - 1
    first_part = own_part == 0
    upper_half = own_part >= n_mesh // 2
    tell({"state": sibling})
    pl.when(jnp.logical_not(last_height))(lambda: tell({"state": towards(0)}))
    pl.when(first_height)(lambda: tell({"state": towards(1)}))
    pl.when(jnp.logical_not(last_part))(lambda: tell({"mesh": above}))
    pl.when(first_part)(lambda: tell({"mesh": below}))
    pl.when(jnp.logical_not(upper_half))(lambda: tell({"mesh": far}))

    loads = [
        pltpu.make_async_copy(rows_hbm, rows_in, local_sem.at[0]),
        pltpu.make_async_copy(sub_hbm.at[pl.ds(128, 128)], raw_part, local_sem.at[1]),
        pltpu.make_async_copy(connect_hbm, connect_in, local_sem.at[2]),
        pltpu.make_async_copy(ham_hbm, ham_in, local_sem.at[3]),
        pltpu.make_async_copy(
            sub_hbm.at[pl.ds(0, 128)], gathered.at[state, pl.ds(0, 128)], local_sem.at[4]
        ),
        pltpu.make_async_copy(ritz_hbm, ritz_in, local_sem.at[5]),
    ]
    for load in loads:
        load.start()
    told = (
        1
        + jnp.minimum(height, 1)
        + lax.div(height, 3)
        + jnp.minimum(own_part, 1)
        + lax.div(own_part, n_mesh - 1)
        + lax.div(own_part, n_mesh // 2)
    )
    pl.semaphore_wait(barrier, told)
    pl.when(jnp.logical_not(first_height))(lambda: answer(0, {"state": towards(1)}))
    pl.when(last_height)(lambda: answer(1, {"state": towards(0)}))
    pl.when(jnp.logical_not(first_part))(lambda: answer(2, {"mesh": below}))
    pl.when(last_part)(lambda: answer(3, {"mesh": above}))
    pl.when(upper_half)(lambda: answer(4, {"mesh": far}))

    def answered(slot):
        return lambda: pl.semaphore_wait(ready.at[slot], 1)

    def span(part, i):
        return pl.ds(pl.multiple_of(128 * part + SIZE * i, SIZE), SIZE)

    def remote(source, target, send_sem, recv_sem, peer):
        return pltpu.make_async_remote_copy(
            src_ref=source,
            dst_ref=target,
            send_sem=send_sem,
            recv_sem=recv_sem,
            device_id={"state": peer},
            device_id_type=MESH,
        )

    def own_copy(part, d, i, owner):
        target = gathered.at[owner, span(part, i)]
        return remote(
            target if part else sub_hbm.at[span(part, i)],
            target,
            own_send.at[part, d, i],
            own_recv.at[part, d, i],
            towards(d),
        )

    def on_copy(part, d, owner):
        target = gathered.at[owner, span(part, d)]
        return remote(
            target, target, on_send.at[part, d], on_recv.at[part, d], towards(d)
        )

    def core_copy(part, kind, i, owner):
        target = gathered.at[owner, span(part, i)]
        return remote(
            target,
            target,
            core_send.at[part, kind, i],
            core_recv.at[part, kind, i],
            sibling,
        )

    def own_sibling(part, owner):
        rows = pl.ds(128 * part, 128)
        target = gathered.at[owner, rows]
        return remote(
            target if part else sub_hbm.at[rows],
            target,
            core_send.at[part, 3, 0],
            core_recv.at[part, 3, 0],
            sibling,
        )

    started = []

    def start(*copies):
        for copy in copies:
            copy.start()
        started.extend(copies)

    a = jnp.minimum(height, 1)
    b = 1 - a
    from_a, from_b = towards(a), towards(b)
    higher = jnp.logical_not(first_height)

    late_first = own_copy(0, b, b, state)
    late_second = own_copy(0, b, a, state)
    pl.when(first_height)(answered(0))
    start(own_copy(0, a, a, state), own_sibling(0, state))
    pl.when(jnp.logical_and(height > 0, height < 3))(answered(0))
    pl.when(higher)(late_first.start)

    def service_first(part):
        for d, owner in ((b, from_a), (a, from_b)):
            own_copy(part, d, d, owner).wait_recv()
            start(on_copy(part, d, owner), core_copy(part, d, d, owner))

    def service_second(part):
        for d, owner in ((b, from_a), (a, from_b)):
            own_copy(part, d, 1 - d, owner).wait_recv()
            start(core_copy(part, d, 1 - d, owner))

    def service_far(part):
        for d in (b, a):
            on_copy(part, d, across).wait_recv()
            start(core_copy(part, 2, d, across))

    def rotate(total, part, owner):
        rows = gathered[owner, 128 * part : 128 * part + 128, :]
        total[...] += dot(ritz_cat[2 * owner + part], right3(rows, 0))

    def rotate_sibling(total, part):
        own_sibling(part, sibling).wait_recv()
        rotate(total, part, sibling)

    def rotate_near(total, part):
        rotate(total, part, from_a)
        rotate(total, part, from_b)

    def rotate_rest(total, part):
        for d, owner in ((b, from_a), (a, from_b)):
            for i in range(2):
                core_copy(part, d, i, owner + flip).wait_recv()
            rotate(total, part, owner + flip)
        rotate(total, part, across)
        for i in range(2):
            core_copy(part, 2, i, across + flip).wait_recv()
        rotate(total, part, across + flip)

    loads[0].wait()
    send_names = jnp.concatenate(
        [rows_in[0, pl.ds(k, 1), :] for k in range(4)], axis=1
    )
    place_f = (
        lax.broadcasted_iota(jnp.int32, (256, 128), 0) == send_names
    ).astype(F32)
    place = place_f.astype(BF16)
    take = jnp.transpose(place_f).astype(BF16)
    take2 = jnp.concatenate([take, take], axis=1)
    place2 = jnp.concatenate([place, place], axis=1)
    take_rows2 = jnp.concatenate([take, take], axis=0)

    def exchange(number):
        copies = []
        for k, (first, count, target, peer) in enumerate(
            ((64, 64, 64, far), (0, 32, 32, above), (32, 32, 0, below))
        ):
            copies.append(
                pltpu.make_async_remote_copy(
                    src_ref=sends.at[number, pl.ds(first, count)],
                    dst_ref=takes.at[number, pl.ds(target, count)],
                    send_sem=halo_send.at[number, k],
                    recv_sem=halo_recv.at[number, k],
                    device_id={"mesh": peer},
                    device_id_type=MESH,
                )
            )
        start(*copies)
        return copies

    centre = 2.5
    sigma_one = 1.5 / (-1.0 - centre)
    sigma_two = 1.0 / (2.0 / sigma_one - sigma_one)
    scale_one = sigma_one / 1.5
    scale_two = 2.0 * sigma_two / 1.5

    class Chain:
        def __init__(self, values, number):
            self.values, self.number, self.copies = values, number, None

        def send(self, value):
            sends[self.number] = value
            self.copies = exchange(self.number)
            self.number += 1

        def arrived(self):
            for copy in self.copies:
                copy.wait_recv()
            return takes[self.number - 1]

        def fetch(self):
            self.send(dot_nt(take2, right2(self.values[...], 1)))

        def apply_first(self):
            self.base = dot_nt(op_cat[...], right3(self.values[...], 1))

        def give_first(self):
            ghosts = right3(self.arrived(), 0)
            self.send(self.base[256:384] + dot(op_gg[...], ghosts))
            self.own = self.base[0:256] + dot(op_og[...], ghosts)
            self.packed = dot(take2, right2(self.own, 0))

        def fetch_second(self):
            back = right2(self.arrived(), 0)
            self.send(scale_one * (self.packed + dot(same2[...], back)))
            first = scale_one * (self.own + dot(place2, back))
            self.base = dot(op_cat[...], right3(first, 0))

        def give_second(self):
            ghosts = right3(self.arrived(), 0)
            self.send(self.base[256:384] + dot(op_gg[...], ghosts))
            own = self.base[0:256] + dot(op_og[...], ghosts)
            self.rest = (
                scale_two * jnp.transpose(own)
                - sigma_one * sigma_two * self.values[...]
            )

        def finish(self):
            back = right2(jnp.transpose(self.arrived()), 1)
            return self.rest + scale_two * dot(back, take_rows2)

    chain = Chain(raw_part, 0)
    loads[1].wait()
    pl.when(jnp.logical_not(last_part))(answered(2))
    pl.when(first_part)(answered(3))
    pl.when(jnp.logical_not(upper_half))(answered(4))
    chain.fetch()
    start(own_copy(0, a, b, state))
    pl.when(higher)(late_second.start)
    started.extend([late_first, late_second])
    same = dot(take, place).astype(BF16)
    same2[...] = jnp.concatenate([same, same], axis=1)

    loads[2].wait()
    connect_pad[...] = jnp.full((16, 128), -1, jnp.int32)
    connect_pad[:, 0:125] = connect_in[...]
    ham_pad[...] = jnp.zeros((16, 128, 128), F32)
    loads[3].wait()
    for e in range(16):
        ham_pad[e, 0:125, 0:125] = ham_in[:, e, :]
    op_sum[...] = jnp.zeros((384, 384), F32)

    def assemble(g, carry):
        picks, spreads = [], []
        for q in range(GROUP):
            e = GROUP * g + q
            names = connect_pad[pl.ds(e, 1), :]
            names = jnp.where(
                names >= 352, names - 32, jnp.where(names >= 320, names + 32, names)
            )
            pick = (
                lax.broadcasted_iota(jnp.int32, (384, 128), 0) == names
            ).astype(F32).astype(BF16)
            high, low = split(ham_pad[e])
            pick2 = jnp.concatenate([pick, pick], axis=1)
            spread = dot_nt(jnp.concatenate([high, low], axis=1), pick2)
            picks.append(pick2)
            spreads.append(right2(spread, 0))
        op_sum[...] += dot(
            jnp.concatenate(picks, axis=1), jnp.concatenate(spreads, axis=0)
        )
        return carry

    lax.fori_loop(0, 16 // GROUP, assemble, 0)

    def start_late():
        pl.semaphore_wait(ready.at[1], 1)
        late_first.start()
        late_second.start()

    pl.when(first_height)(start_late)

    eye = (
        lax.broadcasted_iota(jnp.int32, (384, 256), 0)
        == lax.broadcasted_iota(jnp.int32, (384, 256), 1)
    ).astype(F32)
    op_cat[...] = left3(op_sum[:, 0:256] - centre * eye)
    ghost_cols = left3(op_sum[:, 256:384])
    op_og[...] = ghost_cols[0:256]
    op_gg[...] = ghost_cols[256:384]

    chain.apply_first()
    chain.give_first()
    service_first(0)
    loads[5].wait()
    for i in range(16):
        ritz_cat[i] = left3(ritz_in[:, 128 * i : 128 * i + 128])
    start_acc[...] = jnp.zeros((128, 256), F32)
    out_acc[...] = jnp.zeros((128, 256), F32)
    loads[4].wait()
    rotate(start_acc, 0, state)
    rotate_sibling(start_acc, 0)
    chain.fetch_second()
    service_second(0)
    rotate_near(start_acc, 0)
    chain.give_second()
    service_far(0)
    rotate_rest(start_acc, 0)

    main = Chain(start_acc, 4)
    main.fetch()
    gathered[state, 128:256, :] = chain.finish()
    start(
        own_copy(1, b, b, state),
        own_copy(1, a, a, state),
        own_sibling(1, state),
        own_copy(1, b, a, state),
        own_copy(1, a, b, state),
    )
    main.apply_first()
    main.give_first()
    rotate(out_acc, 1, state)
    main.fetch_second()
    service_first(1)
    rotate_sibling(out_acc, 1)
    main.give_second()
    service_second(1)
    rotate_near(out_acc, 1)
    service_far(1)
    rotate_rest(out_acc, 1)
    out_ref[...] = main.finish() + out_acc[...]

    for copy in started:
        copy.wait_send()


def solution(mesh):
    n_mesh = mesh.shape["mesh"]

    def per_device(subspace, ritz, element_ham, connect, send_rows):
        any_space = pl.BlockSpec(memory_space=pl.ANY)
        hams = jnp.transpose(element_ham, (1, 0, 2))
        return pl.pallas_call(
            functools.partial(kernel, n_mesh),
            out_shape=pltpu.VMEM((128, 256), F32),
            in_specs=[any_space] * 5,
            out_specs=pl.BlockSpec(memory_space=pltpu.VMEM),
            scratch_shapes=[
                pltpu.VMEM((8, 256, 256), F32),
                pltpu.VMEM((128, 2048), F32),
                pltpu.VMEM((16, 128, 384), BF16),
                pltpu.VMEM((125, 16, 125), F32),
                pltpu.VMEM((16, 128, 128), F32),
                pltpu.VMEM((16, 125), jnp.int32),
                pltpu.VMEM((16, 128), jnp.int32),
                pltpu.VMEM((1, 4, 32), jnp.int32),
                pltpu.VMEM((384, 384), F32),
                pltpu.VMEM((384, 768), BF16),
                pltpu.VMEM((128, 384), BF16),
                pltpu.VMEM((256, 384), BF16),
                pltpu.VMEM((128, 256), BF16),
                pltpu.VMEM((128, 256), F32),
                pltpu.VMEM((128, 256), F32),
                pltpu.VMEM((128, 256), F32),
                pltpu.VMEM((8, 128, 128), F32),
                pltpu.VMEM((8, 128, 128), F32),
                pltpu.SemaphoreType.DMA((6,)),
                pltpu.SemaphoreType.REGULAR((5,)),
                pltpu.SemaphoreType.DMA((2, 2, 2)),
                pltpu.SemaphoreType.DMA((2, 2, 2)),
                pltpu.SemaphoreType.DMA((2, 2)),
                pltpu.SemaphoreType.DMA((2, 2)),
                pltpu.SemaphoreType.DMA((2, 4, 2)),
                pltpu.SemaphoreType.DMA((2, 4, 2)),
                pltpu.SemaphoreType.DMA((8, 3)),
                pltpu.SemaphoreType.DMA((8, 3)),
            ],
            compiler_params=pltpu.CompilerParams(
                collective_id=0,
                has_side_effects=True,
                vmem_limit_bytes=60 * 1024 * 1024,
            ),
        )(subspace, ritz, hams, connect, send_rows)

    return jax.shard_map(
        per_device,
        mesh=mesh,
        in_specs=(
            P("state", "mesh"),
            P("state", None),
            P("mesh", None, None),
            P("mesh", None),
            P("mesh", None, None),
        ),
        out_specs=P("state", "mesh"),
        check_vma=False,
    )
```

time: 51.9 us -> 52.7 us (1.015)
  Pallas kernels: 51.1 us -> 51.9 us
    pallas_call x1, Pallas kernels: 51.1 us -> 51.9 us  [per_device(): pl.pallas_call(functools.partial(kernel, n_mesh), out_shape=pltpu.VMEM((1...]
where the time goes in v4:
time: 52.7 us; the launch traced here: 52.6 us
  Pallas kernels  51.9 us (98%)
  local copies, waits for them, and re-layouts  0.66 us (1%)
    pallas_call x1, Pallas kernels, per_device(): pl.pallas_call(functools.partial(kernel, n_mesh), out_shape=pltpu.VMEM((1...  51.9 us

profile of v4, /device:TPU:1, one launch (start us, length us, event | category | flops | bytes accessed | tf_op | source)
XLA Modules:
  0.0 52.6 jit_solution(1564345282581968376)
XLA Ops:
  0.0 51.9 %shard_map.55 = f32[128,256]{1,0:T(8,128)S(1)} custom-call(f32[256,256]{1,0:T(8,128)} %sub_hbm.1, f32[128,2048]{1,0:T(8,128)} %ritz_hbm.1, f32[125,16,125]{2,1,0:T(8,128)} %bitcast.1, s32[16,125]{1,0:T(8,128)} %connect_hbm.1, s32[1,4,32]{2,1,0:T(4,128)} %rows_hbm.1), custom_call_target="tpu_custom_call" | custom-call | tf_op jit(solution)/shard_map/pallas_call | solution.py:450
  51.9 0.7 %copy.7 = f32[128,256]{1,0:T(8,128)} copy(f32[128,256]{1,0:T(8,128)S(1)} %shard_map.55) | data formatting | bytes 262144
